TPU v7x, 32 devices: a whole 2x2x4 slice. The times are simulated.
32 devices in a mesh: section: 4 (over x, core), expert: 8 (over z, y).
Axes of the slice: x: 2, y: 2, z: 4, core: 2. Of those that a mesh axis runs over, the one named last changes fastest.
Arguments:
- sent_acts: bfloat16 [4, 512, 2048], P('section', 'expert'), may hold values from -6 to 6
- stash: bfloat16 [4, 512, 2048], P('section', 'expert'), may hold values from -6 to 6
- cotangents: bfloat16 [4, 512, 2048], P('section', 'expert'), may hold values from -6 to 6
- norm_gain: bfloat16 [4, 2048], P('section'), may hold values from 0.5 to 1.5
- w_gate: bfloat16 [4, 16, 2048, 768], P('section', 'expert'), may hold values from -0.125 to 0.125
- w_up: bfloat16 [4, 16, 2048, 768], P('section', 'expert'), may hold values from -0.125 to 0.125
- w_down: bfloat16 [4, 16, 768, 2048], P('section', 'expert'), may hold values from -0.21875 to 0.21875
- routes_next: int32 [4, 512, 8], P('section', 'expert'), may hold values from 0 to 15, all different within a row; in each aligned block of 64 rows (0 to 63, 64 to 127, ..., all dimensions but the last counted through in order) at most 48 rows name the same one
- gates_next: bfloat16 [4, 512, 8], P('section', 'expert'), may hold values from 0.049804688 to 0.5
- routes_prev: int32 [4, 512, 8], P('section', 'expert'), may hold values from 0 to 15, all different within a row; in each aligned block of 64 rows (0 to 63, 64 to 127, ..., all dimensions but the last counted through in order) at most 48 rows name the same one
- gates_prev: bfloat16 [4, 512, 8], P('section', 'expert'), may hold values from 0.049804688 to 0.5
Outputs:
- fwd_out: bfloat16 [4, 512, 2048], P('section', 'expert')
- bwd_out: bfloat16 [4, 512, 2048], P('section', 'expert')
- gate_grad: bfloat16 [4, 512, 8], P('section', 'expert')
- grad_w_gate: bfloat16 [4, 16, 2048, 768], P('section', 'expert')
- grad_w_up: bfloat16 [4, 16, 2048, 768], P('section', 'expert')
- grad_w_down: bfloat16 [4, 16, 768, 2048], P('section', 'expert')
Inputs may be any that keep to these rules, and one draw needn't show every extreme that they name: `routes_next`: each row names 8 different experts. At most 48 of the 64 tokens of one device choose one expert, and in some device's tokens some expert is chosen by exactly 48. `routes_prev`: each row names 8 different experts. At most 48 of the 64 tokens of one device choose one expert, and in some device's tokens some expert is chosen by exactly 48.
All inputs are finite; a program needn't handle non-finite values.
Results may differ from a plain program's by a relative error of at most 0.008.
Values may be sent and summed in bfloat16 or wider, within the bound.
A program may use at most 128 MiB of HBM per device.

v0:
```python
import jax
import jax.numpy as jnp
from jax import lax
from jax.sharding import PartitionSpec as P

CAP = 48


EPS = 1e-06


def shifted(array, axis, by):
    count = lax.axis_size(axis)
    return lax.ppermute(array, axis, [(i, (i + by) % count) for i in range(count)])


def apply_rms_norm(rows, norm_scale_weight):
    value_entries = rows.astype(jnp.float32)
    inverse_root_scale = lax.rsqrt(
        jnp.mean(value_entries * value_entries, axis=-1, keepdims=True) + EPS
    )
    unit_rows = value_entries * inverse_root_scale
    normalized_rows = (unit_rows * norm_scale_weight.astype(jnp.float32)).astype(jnp.bfloat16)
    return (normalized_rows, unit_rows, inverse_root_scale)


def routing_tables(routes, experts_all):
    tokens_here, top = routes.shape
    flat = routes.reshape(-1)
    onehot = (flat[:, None] == jnp.arange(experts_all, dtype=jnp.int32)[None, :]).astype(jnp.int32)
    before = jnp.cumsum(onehot, axis=0) - onehot
    slot = jnp.sum(before * onehot, axis=1)
    target = flat * CAP + slot
    pick = (target[:, None] == jnp.arange(experts_all * CAP, dtype=jnp.int32)[None, :]).astype(
        jnp.float32
    )
    spread = jnp.sum(pick.reshape(tokens_here, top, -1), axis=1)
    return (pick, spread)


def pack_rows(spread, rows, experts_all, owners):
    packed = jnp.einsum(
        "tr,td->rd", spread.astype(jnp.bfloat16), rows, preferred_element_type=jnp.float32
    ).astype(jnp.bfloat16)
    return packed.reshape(owners, experts_all // owners, CAP, rows.shape[1])


def slot_values(pick, values):
    return jnp.dot(values.reshape(-1).astype(jnp.float32), pick, precision=lax.Precision.HIGHEST)


def choice_values(pick, values, top):
    return jnp.dot(pick, values.reshape(-1), precision=lax.Precision.HIGHEST).reshape(-1, top)


def expert_inputs(rows, weight_gate, weight_up):
    pre_gate = jnp.einsum("sjcd,jdf->sjcf", rows, weight_gate, preferred_element_type=jnp.float32)
    pre_up = jnp.einsum("sjcd,jdf->sjcf", rows, weight_up, preferred_element_type=jnp.float32)
    return (pre_gate, pre_up)


def expert_outputs(hidden, weight_down):
    return jnp.einsum(
        "sjcf,jfd->sjcd", hidden, weight_down, preferred_element_type=jnp.float32
    ).astype(jnp.bfloat16)


def per_device(
    sent_acts,
    stash,
    cotangents,
    norm_gain,
    w_gate,
    w_up,
    w_down,
    routes_next,
    gates_next,
    routes_prev,
    gates_prev,
):
    owners = lax.axis_size("expert")
    norm_scale_weight = norm_gain[0]
    weight_gate = w_gate[0]
    weight_up = w_up[0]
    weight_down = w_down[0]
    top = routes_next.shape[2]
    width = norm_scale_weight.shape[0]
    experts_all = weight_gate.shape[0] * owners
    tokens_here = routes_next.shape[1]
    arrived = shifted(sent_acts, "section", 1)[0]
    normalized_rows, _, _ = apply_rms_norm(arrived, norm_scale_weight)
    pick, spread = routing_tables(routes_next[0], experts_all)
    send = pack_rows(spread, normalized_rows, experts_all, owners)
    blend = jnp.sum(
        pick.reshape(tokens_here, top, -1) * gates_next[0].astype(jnp.float32)[..., None], axis=1
    ).astype(jnp.bfloat16)
    pre_gate, pre_up = expert_inputs(
        lax.all_to_all(send, "expert", split_axis=0, concat_axis=0, tiled=True),
        weight_gate,
        weight_up,
    )
    hidden = (jax.nn.silu(pre_gate) * pre_up).astype(jnp.bfloat16)
    returned = lax.all_to_all(
        expert_outputs(hidden, weight_down), "expert", split_axis=0, concat_axis=0, tiled=True
    )
    mixed = jnp.dot(
        blend, returned.reshape(experts_all * CAP, width), preferred_element_type=jnp.float32
    )
    fwd_out = (arrived.astype(jnp.float32) + mixed).astype(jnp.bfloat16)
    received_rows = shifted(cotangents, "section", -1)[0]
    previous_normalized_rows, unit_rows, inverse_root_scale = apply_rms_norm(
        stash[0], norm_scale_weight
    )
    pick_prev, spread_prev = routing_tables(routes_prev[0], experts_all)
    rows_send = pack_rows(spread_prev, previous_normalized_rows, experts_all, owners)
    plain_send = pack_rows(spread_prev, received_rows, experts_all, owners)
    gate_slots = (
        slot_values(pick_prev, gates_prev[0])
        .astype(jnp.bfloat16)
        .reshape(owners, experts_all // owners, CAP)
    )
    rows_recv, plain_recv, weight_recv = (
        lax.all_to_all(rows_send, "expert", split_axis=0, concat_axis=0, tiled=True),
        lax.all_to_all(plain_send, "expert", split_axis=0, concat_axis=0, tiled=True),
        lax.all_to_all(gate_slots, "expert", split_axis=0, concat_axis=0, tiled=True),
    )
    grad_recv = (
        weight_recv.astype(jnp.float32)[..., None] * plain_recv.astype(jnp.float32)
    ).astype(jnp.bfloat16)
    pre_gate, pre_up = expert_inputs(rows_recv, weight_gate, weight_up)
    sigma = jax.nn.sigmoid(pre_gate)
    active = pre_gate * sigma
    hidden = (active * pre_up).astype(jnp.bfloat16)
    expert_out = expert_outputs(hidden, weight_down)
    d_hidden = jnp.einsum(
        "sjcd,jfd->sjcf", grad_recv, weight_down, preferred_element_type=jnp.float32
    )
    d_gate = (d_hidden * pre_up * sigma * (1.0 + pre_gate * (1.0 - sigma))).astype(jnp.bfloat16)
    d_up = (d_hidden * active).astype(jnp.bfloat16)
    row_grad = (
        jnp.einsum("sjcf,jdf->sjcd", d_gate, weight_gate, preferred_element_type=jnp.float32)
        + jnp.einsum("sjcf,jdf->sjcd", d_up, weight_up, preferred_element_type=jnp.float32)
    ).astype(jnp.bfloat16)
    grad_gate = jnp.einsum(
        "sjcd,sjcf->jdf", rows_recv, d_gate, preferred_element_type=jnp.float32
    ).astype(jnp.bfloat16)
    grad_up = jnp.einsum(
        "sjcd,sjcf->jdf", rows_recv, d_up, preferred_element_type=jnp.float32
    ).astype(jnp.bfloat16)
    grad_down = jnp.einsum(
        "sjcf,sjcd->jfd", hidden, grad_recv, preferred_element_type=jnp.float32
    ).astype(jnp.bfloat16)
    products = jnp.sum(
        expert_out.astype(jnp.float32) * plain_recv.astype(jnp.float32), axis=-1
    ).astype(jnp.bfloat16)
    grad_back, products_back = (
        lax.all_to_all(row_grad, "expert", split_axis=0, concat_axis=0, tiled=True),
        lax.all_to_all(products, "expert", split_axis=0, concat_axis=0, tiled=True),
    )
    gate_grad = choice_values(pick_prev, products_back.astype(jnp.float32), top).astype(
        jnp.bfloat16
    )
    summed = jnp.dot(
        spread_prev.astype(jnp.bfloat16),
        grad_back.reshape(experts_all * CAP, width),
        preferred_element_type=jnp.float32,
    )
    normalized_gradient = summed * norm_scale_weight.astype(jnp.float32)
    backward_result = received_rows.astype(jnp.float32) + inverse_root_scale * (
        normalized_gradient
        - unit_rows * jnp.mean(normalized_gradient * unit_rows, axis=-1, keepdims=True)
    )
    return (
        fwd_out[None],
        backward_result.astype(jnp.bfloat16)[None],
        gate_grad[None],
        grad_gate[None],
        grad_up[None],
        grad_down[None],
    )


def solution(mesh):
    return jax.shard_map(
        per_device,
        mesh=mesh,
        in_specs=(
            P("section", "expert", None),
            P("section", "expert", None),
            P("section", "expert", None),
            P("section", None),
            P("section", "expert", None, None),
            P("section", "expert", None, None),
            P("section", "expert", None, None),
            P("section", "expert", None),
            P("section", "expert", None),
            P("section", "expert", None),
            P("section", "expert", None),
        ),
        out_specs=(
            P("section", "expert", None),
            P("section", "expert", None),
            P("section", "expert", None),
            P("section", "expert", None, None),
            P("section", "expert", None, None),
            P("section", "expert", None, None),
        ),
        check_vma=False,
    )
```

profile of v0, /device:TPU:0, one launch (start us, length us, event | category | flops | bytes accessed | tf_op | source)
XLA Modules:
  0.0 413.2 jit_solution(9998880206730808746)
XLA Ops:
  5.1 7.3 %all-to-all-start.2 = ((bf16[8,2,48]{2,1,0:T(2,128)(2,1)}), bf16[8,2,48]{2,1,0:T(2,128)(2,1)S(1)}, u32[]{:S(2)}, u32[]{:S(2)}) async-start(bf16[8,2,48]{2,1,0:T(2,128)(2,1)} %reshape.169), calls=%async_computation.2 | async-start | bytes 8192 | tf_op jit(solution)/shard_map/all_to_all | solution.py:125
  14.9 3.7 convolution_convert_fusion
  18.9 5.7 %all-to-all-start.4 = ((bf16[8,2,48,2048]{3,2,1,0:T(8,128)(2,1)}), bf16[8,2,48,2048]{3,2,1,0:T(8,128)(2,1)S(1)}, u32[]{:S(2)}, u32[]{:S(2)}) async-start(bf16[8,2,48,2048]{3,2,1,0:T(8,128)(2,1)} %bitcast.29), calls=%async_computation.4 | async-start | bytes 6291456 | tf_op jit(solution)/shard_map/all_to_all | solution.py:123
  24.7 4.2 %collective-permute-done.1 = bf16[1,64,2048]{2,1,0:T(8,128)(2,1)S(1)} collective-permute-done((bf16[1,64,2048]{2,1,0:T(8,128)(2,1)}, bf16[1,64,2048]{2,1,0:T(8,128)(2,1)S(1)}, u32[]{:S(2)}, u32[]{:S(2)}) %collective-permute-start.1) | collective-permute-done | bytes 262176 | tf_op jit(solution)/shard_map/ppermute | solution.py:14
  28.9 2.7 convolution_convert_fusion.1
  31.6 63.2 %all-to-all-done.4 = bf16[8,2,48,2048]{3,2,1,0:T(8,128)(2,1)S(1)} async-done(((bf16[8,2,48,2048]{3,2,1,0:T(8,128)(2,1)}), bf16[8,2,48,2048]{3,2,1,0:T(8,128)(2,1)S(1)}, u32[]{:S(2)}, u32[]{:S(2)}) %all-to-all-start.4) | async-done | bytes 3145760 | tf_op jit(solution)/shard_map/all_to_all | solution.py:123
  94.8 4.6 %all-to-all-start.3 = ((bf16[8,2,48,2048]{3,2,1,0:T(8,128)(2,1)}), bf16[8,2,48,2048]{3,2,1,0:T(8,128)(2,1)}, u32[]{:S(2)}, u32[]{:S(2)}) async-start(bf16[8,2,48,2048]{3,2,1,0:T(8,128)(2,1)} %bitcast.25), calls=%async_computation.3 | async-start | bytes 6291456 | tf_op jit(solution)/shard_map/all_to_all | solution.py:124
  100.9 3.1 reduce-window.14
  110.0 2.4 select_reduce_fusion
  112.6 2.7 convolution_convert_fusion.2
  115.3 54.2 %all-to-all-done.3 = bf16[8,2,48,2048]{3,2,1,0:T(8,128)(2,1)} async-done(((bf16[8,2,48,2048]{3,2,1,0:T(8,128)(2,1)}), bf16[8,2,48,2048]{3,2,1,0:T(8,128)(2,1)}, u32[]{:S(2)}, u32[]{:S(2)}) %all-to-all-start.3) | async-done | bytes 3145760 | tf_op jit(solution)/shard_map/all_to_all | solution.py:124
  169.5 4.6 %all-to-all-start = ((bf16[8,2,48,2048]{3,2,1,0:T(8,128)(2,1)}), bf16[8,2,48,2048]{3,2,1,0:T(8,128)(2,1)}, u32[]{:S(2)}, u32[]{:S(2)}) async-start(bf16[8,2,48,2048]{3,2,1,0:T(8,128)(2,1)} %bitcast.6), calls=%async_computation | async-start | bytes 6291456 | tf_op jit(solution)/shard_map/all_to_all | solution.py:98
  174.2 4.7 %fusion.7 = f32[2,8,48,768]{3,2,1,0:T(8,128)S(1)} fusion(bf16[1,2,2048,768]{3,2,1,0:T(8,128)(2,1)} %param.15, bf16[8,2,48,2048]{3,2,1,0:T(8,128)(2,1)S(1)} %all-to-all-done.4), kind=kOutput, calls=%fused_computation.12 | convolution fusion | flops 2415919104 | bytes 11796480 | tf_op jit(solution)/shard_map/sjcd,jdf->sjcf/dot_general | solution.py:57
  178.9 6.5 %fusion.19 = f32[2,8,48,768]{3,2,1,0:T(8,128)S(1)} fusion(bf16[1,2,768,2048]{3,2,1,0:T(8,128)(2,1)} %param.17, f32[8,2,48]{2,0,1:T(8,128)S(1)} %copy_convert_fusion, bf16[8,2,48,2048]{3,2,1,0:T(8,128)(2,1)} %all-to-all-done.3), kind=kOutput, calls=%fused_computation.24 | convolution fusion | flops 2420637696 | bytes 11799552 | tf_op jit(solution)/shard_map/sjcd,jfd->sjcf/dot_general | solution.py:135
  185.5 7.4 %fusion.50 = (bf16[8,2,48,768]{3,2,0,1:T(8,128)(2,1)S(1)}, bf16[8,2,48,768]{3,2,0,1:T(8,128)(2,1)S(1)}, bf16[8,2,48,768]{3,2,0,1:T(8,128)(2,1)}) fusion(f32[2,8,48,768]{3,2,1,0:T(8,128)S(1)} %fusion.7, f32[2,8,48,768]{3,2,1,0:T(8,128)S(1)} %fusion.19, bf16[1,2,2048,768]{3,2,1,0:T(8,128)(2,1)} %param.16, bf16[8,2,48,2048]{3,2,1,0:T(8,128)(2,1)S(1)} %all-to-all-done.4), kind=kOutput, calls=%fused_computation.52 | convolution fusion | flops 2424766464 | bytes 17694720 | tf_op jit(solution)/shard_map/sjcd,jdf->sjcf/dot_general | solution.py:58
  192.9 5.3 %fusion.1 = bf16[8,2,48]{2,0,1:T(8,128)(2,1)S(1)} fusion(bf16[8,2,48,2048]{3,2,1,0:T(8,128)(2,1)} %all-to-all-done.3, bf16[8,2,48,768]{3,2,0,1:T(8,128)(2,1)S(1)} %get-tuple-element.8, bf16[1,2,768,2048]{3,2,1,0:T(8,128)(2,1)S(1)} %bitcast.239), kind=kOutput, calls=%fused_computation.6 | convolution fusion | flops 2423782656 | bytes 10618368 | tf_op jit(solution)/shard_map/sjcf,jfd->sjcd/dot_general | solution.py:63
  198.8 4.5 %fusion.5 = f32[2,8,48,2048]{3,2,1,0:T(8,128)} fusion(bf16[8,2,48,768]{3,2,0,1:T(8,128)(2,1)S(1)} %get-tuple-element.9, bf16[1,2,2048,768]{3,2,1,0:T(8,128)(2,1)S(1)} %bitcast.237), kind=kOutput, calls=%fused_computation.10 | convolution fusion | flops 2415919104 | bytes 13762560 | tf_op jit(solution)/shard_map/sjcf,jdf->sjcd/dot_general | solution.py:141
  203.3 41.0 %all-to-all-done = bf16[8,2,48,2048]{3,2,1,0:T(8,128)(2,1)} async-done(((bf16[8,2,48,2048]{3,2,1,0:T(8,128)(2,1)}), bf16[8,2,48,2048]{3,2,1,0:T(8,128)(2,1)}, u32[]{:S(2)}, u32[]{:S(2)}) %all-to-all-start) | async-done | bytes 3145760 | tf_op jit(solution)/shard_map/all_to_all | solution.py:98
  244.3 3.5 all-to-all-start.6
  247.8 8.2 %fusion.34 = bf16[8,2,48,2048]{3,2,0,1:T(8,128)(2,1)S(1)} fusion(f32[2,8,48,2048]{3,2,1,0:T(8,128)} %fusion.5, bf16[8,2,48,768]{3,2,0,1:T(8,128)(2,1)S(1)} %copy-done.12, bf16[1,2,2048,768]{3,2,1,0:T(8,128)(2,1)} %param.16), kind=kOutput, calls=%fused_computation.35 | convolution fusion | flops 2419064832 | bytes 16908288 | tf_op jit(solution)/shard_map/sjcf,jdf->sjcd/dot_general | solution.py:142
  257.9 6.0 %all-to-all-start.5 = ((bf16[8,2,48,2048]{3,2,1,0:T(8,128)(2,1)}), bf16[8,2,48,2048]{3,2,1,0:T(8,128)(2,1)S(1)}, u32[]{:S(2)}, u32[]{:S(2)}) async-start(bf16[8,2,48,2048]{3,2,1,0:T(8,128)(2,1)} %copy.161), calls=%async_computation.5 | async-start | bytes 6291456 | tf_op jit(solution)/shard_map/all_to_all | solution.py:157
  263.8 7.7 %fusion.9 = f32[2,8,48,768]{3,2,1,0:T(8,128)} fusion(bf16[1,2,2048,768]{3,2,1,0:T(8,128)(2,1)} %param.15, bf16[8,2,48,2048]{3,2,1,0:T(8,128)(2,1)} %all-to-all-done), kind=kOutput, calls=%fused_computation.14 | convolution fusion | flops 2415919104 | bytes 11796480 | tf_op jit(solution)/shard_map/sjcd,jdf->sjcf/dot_general | solution.py:57
  271.6 13.0 %fusion.31 = bf16[8,2,48,2048]{3,2,0,1:T(8,128)(2,1)} fusion(bf16[1,2,768,2048]{3,2,1,0:T(8,128)(2,1)} %param.17, f32[2,8,48,768]{3,2,1,0:T(8,128)} %fusion.9, bf16[1,2,2048,768]{3,2,1,0:T(8,128)(2,1)} %param.16, bf16[8,2,48,2048]{3,2,1,0:T(8,128)(2,1)} %all-to-all-done), kind=kOutput, calls=%fused_computation.34 | convolution fusion | flops 4836950016 | bytes 21233664 | tf_op jit(solution)/shard_map/sjcf,jfd->sjcd/dot_general | solution.py:63
  284.6 4.0 copy.151
  288.6 45.6 %all-to-all-done.5 = bf16[8,2,48,2048]{3,2,1,0:T(8,128)(2,1)S(1)} async-done(((bf16[8,2,48,2048]{3,2,1,0:T(8,128)(2,1)}), bf16[8,2,48,2048]{3,2,1,0:T(8,128)(2,1)S(1)}, u32[]{:S(2)}, u32[]{:S(2)}) %all-to-all-start.5) | async-done | bytes 3145760 | tf_op jit(solution)/shard_map/all_to_all | solution.py:157
  334.2 4.7 %all-to-all-start.1 = ((bf16[8,2,48,2048]{3,2,1,0:T(8,128)(2,1)}), bf16[8,2,48,2048]{3,2,1,0:T(8,128)(2,1)}, u32[]{:S(2)}, u32[]{:S(2)}) async-start(bf16[8,2,48,2048]{3,2,1,0:T(8,128)(2,1)} %copy.151), calls=%async_computation.1 | async-start | bytes 6291456 | tf_op jit(solution)/shard_map/all_to_all | solution.py:103
  338.9 8.6 %fusion.4 = bf16[1,2,768,2048]{3,2,1,0:T(8,128)(2,1)} fusion(bf16[8,2,48,768]{3,2,0,1:T(8,128)(2,1)} %copy-done.16, f32[8,2,48]{2,0,1:T(8,128)S(1)} %copy_convert_fusion, bf16[8,2,48,2048]{3,2,1,0:T(8,128)(2,1)} %all-to-all-done.3), kind=kOutput, calls=%fused_computation.9 | convolution fusion | flops 2423783424 | bytes 10619904 | tf_op jit(solution)/shard_map/sjcf,sjcd->jfd/dot_general | solution.py:150
  347.6 5.4 %fusion.2 = bf16[1,2,2048,768]{3,2,1,0:T(8,128)(2,1)} fusion(bf16[8,2,48,2048]{3,2,1,0:T(8,128)(2,1)S(1)} %copy-done.2, bf16[8,2,48,768]{3,2,0,1:T(8,128)(2,1)S(1)} %copy-done.15), kind=kOutput, calls=%fused_computation.7 | convolution fusion | flops 2419064832 | bytes 10616832 | tf_op jit(solution)/shard_map/sjcd,sjcf->jdf/dot_general | solution.py:144
  353.0 5.4 %fusion.3 = bf16[1,2,2048,768]{3,2,1,0:T(8,128)(2,1)} fusion(bf16[8,2,48,2048]{3,2,1,0:T(8,128)(2,1)S(1)} %copy-done.2, bf16[8,2,48,768]{3,2,0,1:T(8,128)(2,1)S(1)} %copy-done.13), kind=kOutput, calls=%fused_computation.8 | convolution fusion | flops 2419064832 | bytes 10616832 | tf_op jit(solution)/shard_map/sjcd,sjcf->jdf/dot_general | solution.py:147
  359.1 3.2 fusion.70
  365.3 43.6 %all-to-all-done.1 = bf16[8,2,48,2048]{3,2,1,0:T(8,128)(2,1)} async-done(((bf16[8,2,48,2048]{3,2,1,0:T(8,128)(2,1)}), bf16[8,2,48,2048]{3,2,1,0:T(8,128)(2,1)}, u32[]{:S(2)}, u32[]{:S(2)}) %all-to-all-start.1) | async-done | bytes 3145760 | tf_op jit(solution)/shard_map/all_to_all | solution.py:103
  409.0 3.3 fusion.57
  (92 shorter events, 22.1 us)
Async XLA Ops:
  5.1 13.7 %all-to-all-start.2 = ((bf16[8,2,48]{2,1,0:T(2,128)(2,1)}), bf16[8,2,48]{2,1,0:T(2,128)(2,1)S(1)}, u32[]{:S(2)}, u32[]{:S(2)}) async-start(bf16[8,2,48]{2,1,0:T(2,128)(2,1)} %reshape.169), calls=%async_computation.2 | async-start | bytes 8192 | tf_op jit(solution)/shard_map/all_to_all | solution.py:125
  14.4 4.5 %copy-start.9 = (f32[64]{0:T(128)}, f32[64]{0:T(128)S(1)}, u32[]{:S(2)}) copy-start(f32[64]{0:T(128)S(1)} %add_rsqrt_fusion) | copy-start | bytes 772
  14.4 4.5 %copy-start.7 = (s32[64,8]{1,0:T(8,128)}, s32[64,8]{1,0:T(8,128)S(1)}, u32[]{:S(2)}) copy-start(s32[64,8]{1,0:T(8,128)S(1)} %bitcast_add_fusion) | copy-start | bytes 6148
  18.9 75.9 %all-to-all-start.4 = ((bf16[8,2,48,2048]{3,2,1,0:T(8,128)(2,1)}), bf16[8,2,48,2048]{3,2,1,0:T(8,128)(2,1)S(1)}, u32[]{:S(2)}, u32[]{:S(2)}) async-start(bf16[8,2,48,2048]{3,2,1,0:T(8,128)(2,1)} %bitcast.29), calls=%async_computation.4 | async-start | bytes 6291456 | tf_op jit(solution)/shard_map/all_to_all | solution.py:123
  24.6 4.3 %collective-permute-start.1 = (bf16[1,64,2048]{2,1,0:T(8,128)(2,1)}, bf16[1,64,2048]{2,1,0:T(8,128)(2,1)S(1)}, u32[]{:S(2)}, u32[]{:S(2)}) collective-permute-start(bf16[1,64,2048]{2,1,0:T(8,128)(2,1)} %param.13), channel_id=1, source_target_pairs={{0,24},{8,0},{16,8},{24,16},{1,25},{9,1},{17,9},{25,17},{2,26},{10... | collective-permute-start | bytes 786440 | tf_op jit(solution)/shard_map/ppermute | solution.py:14
  28.9 65.9 %copy-start.5 = (bf16[1,64,2048]{2,1,0:T(8,128)(2,1)}, bf16[1,64,2048]{2,1,0:T(8,128)(2,1)S(1)}, u32[]{:S(2)}) copy-start(bf16[1,64,2048]{2,1,0:T(8,128)(2,1)S(1)} %collective-permute-done.1) | copy-start | bytes 786436
  94.8 90.7 %copy-start.1 = (bf16[8,2,48,2048]{3,2,1,0:T(8,128)(2,1)}, bf16[8,2,48,2048]{3,2,1,0:T(8,128)(2,1)S(1)}, u32[]{:S(2)}) copy-start(bf16[8,2,48,2048]{3,2,1,0:T(8,128)(2,1)S(1)} %all-to-all-done.4) | copy-start | bytes 9437188
  94.8 4.7 %copy-start.11 = (s32[1,64,8]{1,2,0:T(8,128)S(1)}, s32[1,64,8]{1,2,0:T(8,128)}, u32[]{:S(2)}) copy-start(s32[1,64,8]{1,2,0:T(8,128)} %param.18) | copy-start | bytes 6148
  94.8 74.8 %all-to-all-start.3 = ((bf16[8,2,48,2048]{3,2,1,0:T(8,128)(2,1)}), bf16[8,2,48,2048]{3,2,1,0:T(8,128)(2,1)}, u32[]{:S(2)}, u32[]{:S(2)}) async-start(bf16[8,2,48,2048]{3,2,1,0:T(8,128)(2,1)} %bitcast.25), calls=%async_computation.3 | async-start | bytes 6291456 | tf_op jit(solution)/shard_map/all_to_all | solution.py:124
  99.3 13.1 %collective-permute-start = (bf16[1,64,2048]{2,1,0:T(8,128)(2,1)}, bf16[1,64,2048]{2,1,0:T(8,128)(2,1)S(1)}, u32[]{:S(2)}, u32[]{:S(2)}) collective-permute-start(bf16[1,64,2048]{2,1,0:T(8,128)(2,1)} %param.11), channel_id=1, source_target_pairs={{0,8},{8,16},{16,24},{24,0},{1,9},{9,17},{17,25},{25,1},{2,10},{10... | collective-permute-start | bytes 786440 | tf_op jit(solution)/shard_map/ppermute | solution.py:14
  112.5 57.1 %copy-start.3 = (bf16[1,64,2048]{2,1,0:T(8,128)(2,1)}, bf16[1,64,2048]{2,1,0:T(8,128)(2,1)S(1)}, u32[]{:S(2)}) copy-start(bf16[1,64,2048]{2,1,0:T(8,128)(2,1)S(1)} %collective-permute-done) | copy-start | bytes 786436
  169.5 74.7 %all-to-all-start = ((bf16[8,2,48,2048]{3,2,1,0:T(8,128)(2,1)}), bf16[8,2,48,2048]{3,2,1,0:T(8,128)(2,1)}, u32[]{:S(2)}, u32[]{:S(2)}) async-start(bf16[8,2,48,2048]{3,2,1,0:T(8,128)(2,1)} %bitcast.6), calls=%async_computation | async-start | bytes 6291456 | tf_op jit(solution)/shard_map/all_to_all | solution.py:98
  178.9 14.0 %slice-start.2 = ((s8[6291456]{0:T(1024)(128)(4,1)}), s8[4194304]{0:T(1024)(128)(4,1)S(1)}, s32[]{:S(2)}) async-start(s8[6291456]{0:T(1024)(128)(4,1)} %bitcast.238), calls=%async_computation.9 | async-start | bytes 8388608
  178.9 19.9 %slice-start = ((s8[6291456]{0:T(1024)(128)(4,1)}), s8[2097152]{0:T(1024)(128)(4,1)S(1)}, s32[]{:S(2)}) async-start(s8[6291456]{0:T(1024)(128)(4,1)} %bitcast.236), calls=%async_computation.7 | async-start | bytes 4194304
  185.4 7.4 %slice-start.3 = ((s8[6291456]{0:T(1024)(128)(4,1)}), s8[2097152]{0:T(1024)(128)(4,1)S(1)}, s32[]{:S(2)}) async-start(s8[6291456]{0:T(1024)(128)(4,1)} %bitcast.238), calls=%async_computation.10 | async-start | bytes 4194304
  185.5 13.3 %slice-start.1 = ((s8[6291456]{0:T(1024)(128)(4,1)}), s8[4194304]{0:T(1024)(128)(4,1)S(1)}, s32[]{:S(2)}) async-start(s8[6291456]{0:T(1024)(128)(4,1)} %bitcast.236), calls=%async_computation.8 | async-start | bytes 8388608
  192.8 5.3 %copy-start.16 = (bf16[8,2,48,768]{3,2,0,1:T(8,128)(2,1)}, bf16[8,2,48,768]{3,2,0,1:T(8,128)(2,1)S(1)}, u32[]{:S(2)}) copy-start(bf16[8,2,48,768]{3,2,0,1:T(8,128)(2,1)S(1)} %get-tuple-element.8) | copy-start | bytes 3538948
  192.8 5.9 %copy-start.14 = (bf16[8,2,48,768]{3,2,0,1:T(8,128)(2,1)}, bf16[8,2,48,768]{3,2,0,1:T(8,128)(2,1)S(1)}, u32[]{:S(2)}) copy-start(bf16[8,2,48,768]{3,2,0,1:T(8,128)(2,1)S(1)} %get-tuple-element.9) | copy-start | bytes 3538948
  198.8 49.0 %copy-start.12 = (bf16[8,2,48,768]{3,2,0,1:T(8,128)(2,1)S(1)}, bf16[8,2,48,768]{3,2,0,1:T(8,128)(2,1)}, u32[]{:S(2)}) copy-start(bf16[8,2,48,768]{3,2,0,1:T(8,128)(2,1)} %get-tuple-element.10) | copy-start | bytes 3538948
  244.3 13.6 %all-to-all-start.6 = ((bf16[8,2,48]{2,1,0:T(2,128)(2,1)}), bf16[8,2,48]{2,1,0:T(2,128)(2,1)S(1)}, u32[]{:S(2)}, u32[]{:S(2)}) async-start(bf16[8,2,48]{2,1,0:T(2,128)(2,1)} %copy.162), calls=%async_computation.6 | async-start | bytes 8192 | tf_op jit(solution)/shard_map/all_to_all | solution.py:158
  257.9 76.3 %all-to-all-start.5 = ((bf16[8,2,48,2048]{3,2,1,0:T(8,128)(2,1)}), bf16[8,2,48,2048]{3,2,1,0:T(8,128)(2,1)S(1)}, u32[]{:S(2)}, u32[]{:S(2)}) async-start(bf16[8,2,48,2048]{3,2,1,0:T(8,128)(2,1)} %copy.161), calls=%async_computation.5 | async-start | bytes 6291456 | tf_op jit(solution)/shard_map/all_to_all | solution.py:157
  334.2 74.8 %all-to-all-start.1 = ((bf16[8,2,48,2048]{3,2,1,0:T(8,128)(2,1)}), bf16[8,2,48,2048]{3,2,1,0:T(8,128)(2,1)}, u32[]{:S(2)}, u32[]{:S(2)}) async-start(bf16[8,2,48,2048]{3,2,1,0:T(8,128)(2,1)} %copy.151), calls=%async_computation.1 | async-start | bytes 6291456 | tf_op jit(solution)/shard_map/all_to_all | solution.py:103
  338.9 8.7 %copy-start.2 = (bf16[8,2,48,2048]{3,2,1,0:T(8,128)(2,1)S(1)}, bf16[8,2,48,2048]{3,2,1,0:T(8,128)(2,1)}, u32[]{:S(2)}) copy-start(bf16[8,2,48,2048]{3,2,1,0:T(8,128)(2,1)} %copy-done.1) | copy-start | bytes 9437188
  338.9 8.7 %copy-start.15 = (bf16[8,2,48,768]{3,2,0,1:T(8,128)(2,1)S(1)}, bf16[8,2,48,768]{3,2,0,1:T(8,128)(2,1)}, u32[]{:S(2)}) copy-start(bf16[8,2,48,768]{3,2,0,1:T(8,128)(2,1)} %copy-done.14) | copy-start | bytes 3538948
  347.6 5.4 %copy-start.13 = (bf16[8,2,48,768]{3,2,0,1:T(8,128)(2,1)S(1)}, bf16[8,2,48,768]{3,2,0,1:T(8,128)(2,1)}, u32[]{:S(2)}) copy-start(bf16[8,2,48,768]{3,2,0,1:T(8,128)(2,1)} %get-tuple-element.10) | copy-start | bytes 3538948
  353.0 6.1 %copy-start.8 = (s32[64,8]{1,0:T(8,128)S(1)}, s32[64,8]{1,0:T(8,128)}, u32[]{:S(2)}) copy-start(s32[64,8]{1,0:T(8,128)} %copy-done.7) | copy-start | bytes 6148
  353.0 10.7 %copy-start = (bf16[1,64,2048]{2,1,0:T(8,128)(2,1)S(1)}, bf16[1,64,2048]{2,1,0:T(8,128)(2,1)}, u32[]{:S(2)}) copy-start(bf16[1,64,2048]{2,1,0:T(8,128)(2,1)} %param.12) | copy-start | bytes 786436
  353.0 10.7 %copy-start.10 = (f32[64]{0:T(128)S(1)}, f32[64]{0:T(128)}, u32[]{:S(2)}) copy-start(f32[64]{0:T(128)} %copy-done.9) | copy-start | bytes 772
  365.3 47.0 %copy-start.4 = (f32[64,2048]{1,0:T(8,128)S(1)}, f32[64,2048]{1,0:T(8,128)}, u32[]{:S(2)}) copy-start(f32[64,2048]{1,0:T(8,128)} %get-tuple-element.12) | copy-start | bytes 1572868
  365.3 47.0 %copy-start.6 = (bf16[1,64,2048]{2,1,0:T(8,128)(2,1)S(1)}, bf16[1,64,2048]{2,1,0:T(8,128)(2,1)}, u32[]{:S(2)}) copy-start(bf16[1,64,2048]{2,1,0:T(8,128)(2,1)} %copy-done.5) | copy-start | bytes 786436
where the time goes:
time: 415 us; the launch traced here: 413 us
  waiting for transfers between devices  252 us (61%)
  matrix products  94.3 us (23%)
  starting transfers between devices  36.6 us (9%)
  local copies, waits for them, and re-layouts  14.7 us (4%)
  other arithmetic  14.6 us (4%)
    all_to_all x1, waiting for transfers between devices, per_device(): lax.all_to_all(rows_send, 'expert', split_axis=0, concat_axis=0, tiled=True)  63.2 us
    all_to_all x1, waiting for transfers between devices, per_device(): lax.all_to_all(plain_send, 'expert', split_axis=0, concat_axis=0, tiled=T...  54.2 us
    all_to_all x1, waiting for transfers between devices, per_device(): lax.all_to_all(row_grad, 'expert', split_axis=0, concat_axis=0, tiled=True)  45.6 us
    all_to_all x1, waiting for transfers between devices, per_device(): lax.all_to_all(expert_outputs(hidden, weight_down), 'expert', split_axis=...  43.6 us
    all_to_all x1, waiting for transfers between devices, per_device(): lax.all_to_all(send, 'expert', split_axis=0, concat_axis=0, tiled=True)  41 us
    dot_general x2, matrix products, expert_outputs(): jnp.einsum('sjcf,jfd->sjcd', hidden, weight_down, preferred_element_type=...  18.3 us
    dot_general x2, matrix products, expert_inputs(): jnp.einsum('sjcd,jdf->sjcf', rows, weight_gate, preferred_element_type=jn...  12.4 us
    dot_general x3, matrix products, pack_rows(): jnp.einsum('tr,td->rd', spread.astype(jnp.bfloat16), rows, preferred_elem...  9.02 us
  transfers between devices with their start and end apart: 9, of which 7 were waited for; matrix products, arithmetic and copies ran while one was open for 28% of the time, Pallas kernels for 0%

commit v1 on v0

v1 whole, which is shorter than its diff:
```python
import jax
import jax.numpy as jnp
from jax import lax
from jax.sharding import PartitionSpec as P

EPS = 1e-06
F32 = jnp.float32
BF16 = jnp.bfloat16


def shifted(array, axis, by):
    count = lax.axis_size(axis)
    return lax.ppermute(array, axis, [(i, (i + by) % count) for i in range(count)])


def apply_rms_norm(rows, gain):
    values = rows.astype(F32)
    scale = lax.rsqrt(jnp.mean(values * values, axis=-1, keepdims=True) + EPS)
    unit = values * scale
    return (unit * gain).astype(BF16), unit, scale


def dense_gates(routes, gates, experts_all):
    hit = routes[:, :, None] == jnp.arange(experts_all, dtype=jnp.int32)
    return jnp.sum(jnp.where(hit, gates.astype(F32)[:, :, None], 0.0), axis=1).astype(BF16)


def dot(a, b, ca, cb):
    return lax.dot_general(a, b, (((ca,), (cb,)), ((), ())), preferred_element_type=F32)


def gathered(array):
    return lax.all_gather(array, "expert", axis=0, tiled=True)


def per_device(
    sent_acts,
    stash,
    cotangents,
    norm_gain,
    w_gate,
    w_up,
    w_down,
    routes_next,
    gates_next,
    routes_prev,
    gates_prev,
):
    owners = lax.axis_size("expert")
    me = lax.axis_index("expert")
    gain = norm_gain[0].astype(F32)
    wg, wu, wd = w_gate[0], w_up[0], w_down[0]
    local, width, hidden_units = wg.shape
    experts_all = local * owners
    tokens = stash.shape[1]

    dense = jnp.concatenate(
        [
            dense_gates(routes_next[0], gates_next[0], experts_all),
            dense_gates(routes_prev[0], gates_prev[0], experts_all),
        ],
        axis=1,
    )
    cot = shifted(cotangents, "section", -1)[0]
    arrived = shifted(sent_acts, "section", 1)[0]
    prev_rows, unit_rows, scale = apply_rms_norm(stash[0], gain)
    next_rows, _, _ = apply_rms_norm(arrived, gain)

    dense_all = gathered(dense)
    prev_all = gathered(prev_rows)
    cot_all = gathered(cot)
    next_all = gathered(next_rows)

    mine = lax.dynamic_slice_in_dim(
        dense_all.reshape(-1, 2, owners, local), me, 1, axis=2
    )[:, :, 0].astype(F32)
    gate_next, gate_prev = mine[:, 0], mine[:, 1]

    gated, d_gate, d_up, products, weight_grads = [], [], [], [], []
    for j in range(local):
        pre_gate = dot(prev_all, wg[j], 1, 0)
        pre_up = dot(prev_all, wu[j], 1, 0)
        plain = dot(cot_all, wd[j], 1, 1)
        weight = gate_prev[:, j : j + 1]
        sigma = jax.nn.sigmoid(pre_gate)
        active = pre_gate * sigma
        hidden = active * pre_up
        products.append(jnp.sum(hidden * plain, axis=1))
        d_hidden = weight * plain
        gated.append((weight * hidden).astype(BF16))
        d_gate.append((d_hidden * pre_up * sigma * (1.0 + pre_gate * (1.0 - sigma))).astype(BF16))
        d_up.append((d_hidden * active).astype(BF16))
    row_grad = sum(dot(d_gate[j], wg[j], 1, 1) + dot(d_up[j], wu[j], 1, 1) for j in range(local))
    summed = lax.psum_scatter(row_grad.astype(BF16), "expert", scatter_dimension=0, tiled=True)
    products = jnp.stack(products, axis=1).astype(BF16).reshape(owners, tokens, local)
    products_back = lax.all_to_all(products, "expert", split_axis=0, concat_axis=0, tiled=True)

    mixed = 0.0
    for j in range(local):
        hidden = jax.nn.silu(dot(next_all, wg[j], 1, 0)) * dot(next_all, wu[j], 1, 0)
        mixed = mixed + dot((gate_next[:, j : j + 1] * hidden).astype(BF16), wd[j], 1, 0)
    mixed = lax.psum_scatter(mixed.astype(BF16), "expert", scatter_dimension=0, tiled=True)

    grad_gate = jnp.stack([dot(prev_all, d_gate[j], 0, 0).astype(BF16) for j in range(local)])
    grad_up = jnp.stack([dot(prev_all, d_up[j], 0, 0).astype(BF16) for j in range(local)])
    grad_down = jnp.stack([dot(gated[j], cot_all, 0, 0).astype(BF16) for j in range(local)])

    fwd_out = (arrived.astype(F32) + mixed.astype(F32)).astype(BF16)

    by_expert = jnp.transpose(products_back, (1, 0, 2)).reshape(tokens, experts_all).astype(F32)
    hit = routes_prev[0][:, :, None] == jnp.arange(experts_all, dtype=jnp.int32)
    gate_grad = jnp.sum(jnp.where(hit, by_expert[:, None, :], 0.0), axis=-1).astype(BF16)

    normalized_gradient = summed.astype(F32) * gain
    backward = cot.astype(F32) + scale * (
        normalized_gradient
        - unit_rows * jnp.mean(normalized_gradient * unit_rows, axis=-1, keepdims=True)
    )
    return (
        fwd_out[None],
        backward.astype(BF16)[None],
        gate_grad[None],
        grad_gate[None],
        grad_up[None],
        grad_down[None],
    )


def solution(mesh):
    tokens = P("section", "expert", None)
    weights = P("section", "expert", None, None)
    return jax.shard_map(
        per_device,
        mesh=mesh,
        in_specs=(tokens, tokens, tokens, P("section", None), weights, weights, weights)
        + (tokens,) * 4,
        out_specs=(tokens, tokens, tokens, weights, weights, weights),
        check_vma=False,
    )
```

time: 415 us -> 415 us (level); the launches traced: 413 us -> 407 us
  blocking collectives: 0 us -> 30.7 us
  starting transfers between devices: 36.6 us -> 6.24 us
  between operations: 0.94 us -> 14.6 us
  matrix products: 94.3 us -> 81.9 us
  local copies, waits for them, and re-layouts: 14.7 us -> 4.54 us
  other arithmetic: 14.6 us -> 24.3 us
  waiting for transfers between devices: 252 us -> 245 us
    all_to_all x6 -> x0, waiting for transfers between devices: 248 us -> none  [the longest x1 63.2 us: per_device(): lax.all_to_all(rows_send, 'expert', split_axis=0, concat_axis=0, tiled=True)]
    all_gather x0 -> x3, waiting for transfers between devices: none -> 128 us  [gathered(): return lax.all_gather(array, 'expert', axis=0, tiled=True)]
    reduce_scatter x0 -> x2, waiting for transfers between devices: none -> 100 us  [the longest x1 59.5 us: per_device(): lax.psum_scatter(row_grad.astype(BF16), 'expert', scatter_dimension=0, ti...]
    all_to_all x6 -> x0, starting transfers between devices: 32.9 us -> none  [the longest x1 7.31 us: per_device(): lax.all_to_all(gate_slots, 'expert', split_axis=0, concat_axis=0, tiled=T...]
    all_gather x0 -> x1, blocking collectives: none -> 30.7 us  [gathered(): return lax.all_gather(array, 'expert', axis=0, tiled=True)]
    broadcast_in_dim x1 -> x5, other arithmetic: 0.91 us -> 13.9 us  [the longest x1 3.75 us: per_device(): grad_up[None]]
    dot_general x18 -> x20, matrix products: 94.3 us -> 81.9 us  [dot(): lax.dot_general(a, b, (((ca,), (cb,)), ((), ())), preferred_element_type=...]
    convert_element_type x4 -> x0, local copies, waits for them, and re-layouts: 6.57 us -> none  [the longest x1 4.01 us: expert_outputs(): return jnp.einsum('sjcf,jfd->sjcd', hidden, weight_down, preferred_elemen...]
  transfers between devices with their start and end apart: 9 -> 8, of which waited for: 7 -> 8; matrix products, arithmetic and copies ran while one was open for 28% -> 10% of each run, Pallas kernels for 0% -> 0%
where the time goes in v1:
time: 415 us; the launch traced here: 407 us
  waiting for transfers between devices  245 us (59%)
  matrix products  81.9 us (20%)
  blocking collectives  30.7 us (7%)
  other arithmetic  24.3 us (6%)
  between operations  14.6 us (4%)
  starting transfers between devices  6.24 us (2%)
  local copies, waits for them, and re-layouts  4.54 us (1%)
    all_gather x3, waiting for transfers between devices, gathered(): return lax.all_gather(array, 'expert', axis=0, tiled=True)  128 us
    dot_general x20, matrix products, dot(): lax.dot_general(a, b, (((ca,), (cb,)), ((), ())), preferred_element_type=...  81.9 us
    reduce_scatter x1, waiting for transfers between devices, per_device(): lax.psum_scatter(row_grad.astype(BF16), 'expert', scatter_dimension=0, ti...  59.5 us
    reduce_scatter x1, waiting for transfers between devices, per_device(): lax.psum_scatter(mixed.astype(BF16), 'expert', scatter_dimension=0, tiled...  41 us
    all_gather x1, blocking collectives, gathered(): return lax.all_gather(array, 'expert', axis=0, tiled=True)  30.7 us
    ppermute x2, waiting for transfers between devices, shifted(): lax.ppermute(array, axis, [(i, (i + by) % count) for i in range(count)])  10.2 us
  transfers between devices with their start and end apart: 8, of which 8 were waited for; matrix products, arithmetic and copies ran while one was open for 10% of the time, Pallas kernels for 0%

profile of v1, /device:TPU:0, one launch (start us, length us, event | category | flops | bytes accessed | tf_op | source)
XLA Modules:
  0.0 407.1 jit_solution(16580083818961828982)
XLA Ops:
  10.9 2.5 collective-permute-start.1
  13.4 4.2 %collective-permute-done.1 = bf16[1,64,2048]{2,1,0:T(8,128)(2,1)S(1)} collective-permute-done((bf16[1,64,2048]{2,1,0:T(8,128)(2,1)}, bf16[1,64,2048]{2,1,0:T(8,128)(2,1)S(1)}, u32[]{:S(2)}, u32[]{:S(2)}) %collective-permute-start.1) | collective-permute-done | bytes 262176 | tf_op jit(solution)/shard_map/ppermute | solution.py:13
  19.0 43.8 %all-gather.8.cloned.1.call-done = bf16[512,2048]{1,0:T(8,128)(2,1)} async-done(((bf16[64,2048]{1,0:T(8,128)(2,1)}), bf16[512,2048]{1,0:T(8,128)(2,1)}) %all-gather.8.cloned.1.call-update) | async-done | bytes 2097168 | tf_op jit(solution)/shard_map/all_gather | solution.py:33
  62.8 5.6 %fusion.6 = f32[512,768]{1,0:T(8,128)} fusion(bf16[512,2048]{1,0:T(8,128)(2,1)} %all-gather.8.cloned.1.call-done, bf16[1,2,2048,768]{3,2,1,0:T(8,128)(2,1)} %param.16), kind=kOutput, calls=%fused_computation.17 | convolution fusion | flops 1610612736 | bytes 6815744 | tf_op jit(solution)/shard_map/dot_general | solution.py:29
  68.4 3.9 fusion.22
  72.3 3.0 fusion.12
  77.2 36.0 %all-gather.10.cloned.1.call-done = bf16[1,512,2048]{2,1,0:T(8,128)(2,1)} async-done(((bf16[1,64,2048]{2,1,0:T(8,128)(2,1)}), bf16[1,512,2048]{2,1,0:T(8,128)(2,1)}) %all-gather.10.cloned.1.call-update) | async-done | bytes 2097168 | tf_op jit(solution)/shard_map/all_gather | solution.py:33
  113.2 6.5 %multiply_reduce_fusion = (bf16[512]{0:T(512)(128)(2,1)S(1)}, f32[512,768]{1,0:T(8,128)}) fusion(f32[512,768]{1,0:T(8,128)} %fusion.6, f32[512,768]{1,0:T(8,128)} %fusion.12, bf16[1,2,768,2048]{3,2,1,0:T(8,128)(2,1)} %param.17, bf16[1,512,2048]{2,1,0:T(8,128)(2,1)} %all-gather.10.cloned.1.call-done), kind=kOutput, calls=%fused_computation.71 | convolution fusion | flops 1613364736 | bytes 9962496 | tf_op jit(solution)/shard_map/dot_general | solution.py:29
  119.7 5.7 %multiply_reduce_fusion.1 = (bf16[512]{0:T(512)(128)(2,1)S(1)}, f32[512,768]{1,0:T(8,128)}) fusion(f32[512,768]{1,0:T(8,128)S(1)} %fusion.22, f32[512,768]{1,0:T(8,128)S(1)} %fusion.28, bf16[1,2,768,2048]{3,2,1,0:T(8,128)(2,1)} %param.17, bf16[1,512,2048]{2,1,0:T(8,128)(2,1)} %all-gather.10.cloned.1.call-done), kind=kOutput, calls=%fused_computation.72 | convolution fusion | flops 1613364736 | bytes 9962496 | tf_op jit(solution)/shard_map/dot_general | solution.py:29
  126.1 3.3 all-to-all-start
  129.5 6.3 %all-to-all-done = bf16[8,64,2]{1,2,0:T(2,128)(2,1)S(1)} async-done(((bf16[8,64,2]{1,2,0:T(2,128)(2,1)}), bf16[8,64,2]{1,2,0:T(2,128)(2,1)S(1)}, u32[]{:S(2)}, u32[]{:S(2)}) %all-to-all-start) | async-done | bytes 2080 | tf_op jit(solution)/shard_map/all_to_all | solution.py:96
  136.4 30.7 %all-gather.1 = bf16[8,64,32]{1,2,0:T(8,128)(2,1)S(1)} all-gather(bf16[1,64,32]{1,2,0:T(8,128)(2,1)S(1)} %maximum_bitcast_fusion.3), channel_id=1, replica_groups=mesh['section'=4,'expert'=8] {'expert'}, dimensions={0}, use_global_device_ids=true | all-gather | bytes 36864 | tf_op jit(solution)/shard_map/all_gather | solution.py:33
  167.3 3.3 multiply_convert_fusion.2
  170.6 4.3 %fusion.10 = f32[512,2048]{1,0:T(8,128)S(1)} fusion(bf16[512,768]{1,0:T(8,128)(2,1)S(1)} %get-tuple-element.11, bf16[1,2,2048,768]{3,2,1,0:T(8,128)(2,1)} %param.15), kind=kOutput, calls=%fused_computation.21 | convolution fusion | flops 1610612736 | bytes 8126464 | tf_op jit(solution)/shard_map/dot_general | solution.py:29
  180.1 3.2 add_convert_fusion
  183.5 6.0 %collective-permute-done = bf16[1,64,2048]{2,1,0:T(8,128)(2,1)S(1)} collective-permute-done((bf16[1,64,2048]{2,1,0:T(8,128)(2,1)}, bf16[1,64,2048]{2,1,0:T(8,128)(2,1)S(1)}, u32[]{:S(2)}, u32[]{:S(2)}) %collective-permute-start) | collective-permute-done | bytes 262176 | tf_op jit(solution)/shard_map/ppermute | solution.py:13
  189.6 59.5 %reduce-scatter.5.cloned.1.call-done = bf16[64,2048]{1,0:T(8,128)(2,1)} async-done(((bf16[512,2048]{1,0:T(8,128)(2,1)}), bf16[64,2048]{1,0:T(8,128)(2,1)}) %reduce-scatter.5.cloned.1.call-update) | async-done | bytes 262160 | tf_op jit(solution)/shard_map/reduce_scatter | solution.py:94
  250.4 2.0 fusion.95
  252.6 48.0 %all-gather.6.cloned.1.call-done = bf16[512,2048]{1,0:T(8,128)(2,1)} async-done(((bf16[64,2048]{1,0:T(8,128)(2,1)}), bf16[512,2048]{1,0:T(8,128)(2,1)}) %all-gather.6.cloned.1.call-update) | async-done | bytes 2097168 | tf_op jit(solution)/shard_map/all_gather | solution.py:33
  300.6 5.6 %fusion.14 = f32[512,768]{1,0:T(8,128)} fusion(bf16[512,2048]{1,0:T(8,128)(2,1)} %all-gather.6.cloned.1.call-done, bf16[1,2,2048,768]{3,2,1,0:T(8,128)(2,1)} %param.15), kind=kOutput, calls=%fused_computation.25 | convolution fusion | flops 1610612736 | bytes 6815744 | tf_op jit(solution)/shard_map/dot_general | solution.py:29
  306.2 4.9 %fusion.30 = f32[512,768]{1,0:T(8,128)} fusion(bf16[512,2048]{1,0:T(8,128)(2,1)S(1)} %copy-done.21, bf16[1,2,2048,768]{3,2,1,0:T(8,128)(2,1)} %param.15), kind=kOutput, calls=%fused_computation.41 | convolution fusion | flops 1610612736 | bytes 6815744 | tf_op jit(solution)/shard_map/dot_general | solution.py:29
  311.1 9.9 %fusion.2 = f32[512,2048]{1,0:T(8,128)} fusion(bf16[1,2,768,2048]{3,2,1,0:T(8,128)(2,1)} %param.17, f32[512,768]{1,0:T(8,128)} %fusion.14, bf16[512,2048]{1,0:T(8,128)(2,1)} %all-gather.6.cloned.1.call-done, bf16[1,2,2048,768]{3,2,1,0:T(8,128)(2,1)} %param.16, f32[512]{0:T(512)S(1)} %bitcast.169), kind=kOutput, calls=%fused_computation.13 | convolution fusion | flops 3223977984 | bytes 14157824 | tf_op jit(solution)/shard_map/dot_general | solution.py:29
  320.9 10.4 %add_convert_fusion.1 = bf16[512,2048]{1,0:T(8,128)(2,1)} fusion(f32[512,2048]{1,0:T(8,128)} %fusion.2, bf16[1,2,768,2048]{3,2,1,0:T(8,128)(2,1)} %param.17, f32[512,768]{1,0:T(8,128)} %fusion.30, bf16[512,2048]{1,0:T(8,128)(2,1)} %all-gather.6.cloned.1.call-done, bf16[1,2,2048,768]{3,2,1,0:T(8,128)(2,1)} %param.16, f32[512]{0:T(512)S(1)} %bitcast.168), kind=kOutput, calls=%fused_computation.4 | convolution fusion | flops 3226075136 | bytes 16254976 | tf_op jit(solution)/shard_map/dot_general | solution.py:29
  332.5 3.6 fusion.33
  336.1 2.1 fusion.32
  338.3 3.2 maximum_bitcast_fusion
  341.5 1.9 fusion.35
  345.3 3.7 maximum_bitcast_fusion.1
  350.1 2.0 fusion.37
  352.2 2.1 fusion.36
  354.3 3.2 maximum_bitcast_fusion.2
  357.5 41.0 %reduce-scatter.3.cloned.1.call-done = bf16[64,2048]{1,0:T(8,128)(2,1)} async-done(((bf16[512,2048]{1,0:T(8,128)(2,1)}), bf16[64,2048]{1,0:T(8,128)(2,1)}) %reduce-scatter.3.cloned.1.call-update) | async-done | bytes 262160 | tf_op jit(solution)/shard_map/reduce_scatter | solution.py:102
  (99 shorter events, 21.2 us)
Async XLA Ops:
  7.2 55.7 %all-gather.8.cloned.1.call-start = ((), (), s32[]{:S(2)}) async-start(), calls=%async_computation.5 | async-start | bytes 2359296 | tf_op jit(solution)/shard_map/all_gather | solution.py:33
  10.9 102.3 %all-gather.10.cloned.1.call-start = ((), (), s32[]{:S(2)}) async-start(), calls=%async_computation.7 | async-start | bytes 2359296 | tf_op jit(solution)/shard_map/all_gather | solution.py:33
  10.9 6.7 %collective-permute-start.1 = (bf16[1,64,2048]{2,1,0:T(8,128)(2,1)}, bf16[1,64,2048]{2,1,0:T(8,128)(2,1)S(1)}, u32[]{:S(2)}, u32[]{:S(2)}) collective-permute-start(bf16[1,64,2048]{2,1,0:T(8,128)(2,1)} %param.13), channel_id=1, source_target_pairs={{0,24},{8,0},{16,8},{24,16},{1,25},{9,1},{17,9},{25,17},{2,26},{10... | collective-permute-start | bytes 786440 | tf_op jit(solution)/shard_map/ppermute | solution.py:13
  62.8 5.6 %copy-start.18 = (bf16[512,2048]{1,0:T(8,128)(2,1)S(1)}, bf16[512,2048]{1,0:T(8,128)(2,1)}, u32[]{:S(2)}) copy-start(bf16[512,2048]{1,0:T(8,128)(2,1)} %all-gather.8.cloned.1.call-done) | copy-start | bytes 6291460
  62.8 9.5 %slice-start = ((s8[6291456]{0:T(1024)(128)(4,1)}), s8[4194304]{0:T(1024)(128)(4,1)S(1)}, s32[]{:S(2)}) async-start(s8[6291456]{0:T(1024)(128)(4,1)} %bitcast.153), calls=%async_computation.8 | async-start | bytes 8388608
  68.4 3.9 slice-start.1
  77.2 42.5 %copy-start.1 = (f32[512,768]{1,0:T(8,128)}, f32[512,768]{1,0:T(8,128)S(1)}, u32[]{:S(2)}) copy-start(f32[512,768]{1,0:T(8,128)S(1)} %fusion.28) | copy-start | bytes 4718596
  119.7 9.7 %copy-start.17 = (bf16[1,64,8]{1,2,0:T(8,128)(2,1)S(1)}, bf16[1,64,8]{1,2,0:T(8,128)(2,1)}, u32[]{:S(2)}) copy-start(bf16[1,64,8]{1,2,0:T(8,128)(2,1)} %param.19) | copy-start | bytes 3076
  119.7 16.0 %copy-start.15 = (s32[1,64,8]{1,2,0:T(8,128)S(1)}, s32[1,64,8]{1,2,0:T(8,128)}, u32[]{:S(2)}) copy-start(s32[1,64,8]{1,2,0:T(8,128)} %param.20) | copy-start | bytes 6148
  119.7 16.0 %copy-start.16 = (s32[1,64,8]{1,2,0:T(8,128)S(1)}, s32[1,64,8]{1,2,0:T(8,128)}, u32[]{:S(2)}) copy-start(s32[1,64,8]{1,2,0:T(8,128)} %param.18) | copy-start | bytes 6148
  126.1 9.7 %all-to-all-start = ((bf16[8,64,2]{1,2,0:T(2,128)(2,1)}), bf16[8,64,2]{1,2,0:T(2,128)(2,1)S(1)}, u32[]{:S(2)}, u32[]{:S(2)}) async-start(bf16[8,64,2]{1,2,0:T(2,128)(2,1)} %copy.42), calls=%async_computation.2 | async-start | bytes 8192 | tf_op jit(solution)/shard_map/all_to_all | solution.py:96
  129.4 119.8 %reduce-scatter.5.cloned.1.call-start = ((), (), s32[]{:S(2)}) async-start(), calls=%async_computation.6 | async-start | bytes 2359296 | tf_op jit(solution)/shard_map/reduce_scatter | solution.py:94
  167.3 7.6 %slice-start.4 = ((s8[6291456]{0:T(1024)(128)(4,1)}), s8[4194304]{0:T(1024)(128)(4,1)S(1)}, s32[]{:S(2)}) async-start(s8[6291456]{0:T(1024)(128)(4,1)} %bitcast.170), calls=%async_computation.12 | async-start | bytes 8388608
  170.5 4.4 %copy-start.11 = (bf16[512,768]{1,0:T(8,128)(2,1)}, bf16[512,768]{1,0:T(8,128)(2,1)S(1)}, u32[]{:S(2)}) copy-start(bf16[512,768]{1,0:T(8,128)(2,1)S(1)} %get-tuple-element.11) | copy-start | bytes 2359300
  170.6 4.4 %copy-start.9 = (bf16[512,768]{1,0:T(8,128)(2,1)}, bf16[512,768]{1,0:T(8,128)(2,1)S(1)}, u32[]{:S(2)}) copy-start(bf16[512,768]{1,0:T(8,128)(2,1)S(1)} %get-tuple-element.10) | copy-start | bytes 2359300
  170.6 4.4 %slice-start.5 = ((s8[6291456]{0:T(1024)(128)(4,1)}), s8[2097152]{0:T(1024)(128)(4,1)S(1)}, s32[]{:S(2)}) async-start(s8[6291456]{0:T(1024)(128)(4,1)} %bitcast.170), calls=%async_computation.13 | async-start | bytes 4194304
  174.9 1.9 copy-start.6
  176.8 2.7 slice-start.2
  177.6 2.5 slice-start.3
  183.3 65.8 %copy-start = (bf16[1,64,2048]{2,1,0:T(8,128)(2,1)S(1)}, bf16[1,64,2048]{2,1,0:T(8,128)(2,1)}, u32[]{:S(2)}) copy-start(bf16[1,64,2048]{2,1,0:T(8,128)(2,1)} %param.12) | copy-start | bytes 786436
  183.3 67.0 %copy-start.8 = (bf16[1,64,2048]{2,1,0:T(8,128)(2,1)S(1)}, bf16[1,64,2048]{2,1,0:T(8,128)(2,1)}, u32[]{:S(2)}) copy-start(bf16[1,64,2048]{2,1,0:T(8,128)(2,1)} %copy-done.7) | copy-start | bytes 786436
  183.3 117.3 %all-gather.6.cloned.1.call-start = ((), (), s32[]{:S(2)}) async-start(), calls=%async_computation.3 | async-start | bytes 2359296 | tf_op jit(solution)/shard_map/all_gather | solution.py:33
  183.4 6.1 %collective-permute-start = (bf16[1,64,2048]{2,1,0:T(8,128)(2,1)}, bf16[1,64,2048]{2,1,0:T(8,128)(2,1)S(1)}, u32[]{:S(2)}, u32[]{:S(2)}) collective-permute-start(bf16[1,64,2048]{2,1,0:T(8,128)(2,1)} %param.11), channel_id=1, source_target_pairs={{0,8},{8,16},{16,24},{24,0},{1,9},{9,17},{17,25},{25,1},{2,10},{10... | collective-permute-start | bytes 786440 | tf_op jit(solution)/shard_map/ppermute | solution.py:13
  252.3 146.1 %reduce-scatter.3.cloned.1.call-start = ((), (), s32[]{:S(2)}) async-start(), calls=%async_computation.4 | async-start | bytes 2359296 | tf_op jit(solution)/shard_map/reduce_scatter | solution.py:102
  300.6 5.6 %copy-start.21 = (bf16[512,2048]{1,0:T(8,128)(2,1)S(1)}, bf16[512,2048]{1,0:T(8,128)(2,1)}, u32[]{:S(2)}) copy-start(bf16[512,2048]{1,0:T(8,128)(2,1)} %all-gather.6.cloned.1.call-done) | copy-start | bytes 6291460
  332.5 3.6 copy-start.19
  338.3 3.3 copy-start.10
  341.5 1.9 copy-start.14
  345.3 3.8 copy-start.4
  345.3 3.8 copy-start.5
  345.3 4.8 %copy-start.20 = (bf16[1,512,2048]{2,1,0:T(8,128)(2,1)S(1)}, bf16[1,512,2048]{2,1,0:T(8,128)(2,1)}, u32[]{:S(2)}) copy-start(bf16[1,512,2048]{2,1,0:T(8,128)(2,1)} %all-gather.10.cloned.1.call-done) | copy-start | bytes 6291460
  350.1 2.1 copy-start.3
  (4 other events, 5.5 us)
Sparse Core Ops, SparseCore 0:
  11.0 51.7 all-gather.7
  65.5 47.6 all-gather.9
  183.5 65.6 reduce-scatter.4
  252.5 48.0 all-gather.5
  331.5 66.8 reduce-scatter.2
